TPU v7x, 32 devices: a whole 2x2x4 slice. The times are simulated.
32 devices in a mesh: row: 8 (over z, y), col: 4 (over x, core).
Axes of the slice: x: 2, y: 2, z: 4, core: 2. Of those that a mesh axis runs over, the one named last changes fastest.
Arguments:
- tile_basis: bfloat16 [8, 4, 2304, 256], P('row', 'col'), may hold values from -6 to 6
- tile_coeffs: bfloat16 [8, 4, 2304, 256], P('row', 'col'), may hold values from -0.375 to 0.375
- panel_basis: bfloat16 [8, 256, 2304], P('row', 'col'), may hold values from -6 to 6
- panel_coeffs: bfloat16 [8, 256, 2304], P('row', 'col'), may hold values from -0.125 to 0.125
- tile_rank: int32 [8, 4], P('row', 'col'), may hold values from 64 to 256
- target_rank: int32 [8, 4], P('row', 'col'), may hold values from 64 to 256, as said below
- panel_rank: int32 [8], replicated, may hold values from 64 to 256
- owner_row: int32 [4], replicated, may hold values from 0 to 7, as said below
Outputs:
- fresh_basis: bfloat16 [8, 4, 2304, 256], P('row', 'col')
- fresh_coeffs: bfloat16 [8, 4, 2304, 256], P('row', 'col')
Inputs may be any that keep to these rules, and one draw needn't show every extreme that they name: `target_rank`: a tile's rank after recompression never exceeds its rank before. `owner_row`: distinct panel tile rows.
All inputs are finite; a program needn't handle non-finite values.
Results may differ from a plain program's by a relative error of at most 0.0068.
Values may be sent and summed in bfloat16 or wider, within the bound.
No kernel may reach another device: no remote copies, remote signals or barrier semaphores. Data moves between devices by JAX's collectives and lax.ppermute only.
A program may use at most 64 MiB of HBM per device.

v0:
```python
import math
import jax
import jax.numpy as jnp
from jax import lax
from jax.sharding import PartitionSpec as P

NB = 2304


def spread(value, axis, source):
    kept = jnp.where(lax.axis_index(axis) == source, value, 0).astype(value.dtype)
    return lax.psum(kept, axis)


def keep_columns(matrix, limit):
    flags = (jnp.arange(matrix.shape[1]) < limit).astype(matrix.dtype)
    return matrix * flags[None, :]


def keep_rows(matrix, limit):
    flags = (jnp.arange(matrix.shape[0]) < limit).astype(matrix.dtype)
    return matrix * flags[:, None]


def lead_product(first, second):
    return lax.dot_general(
        first, second, (((0,), (0,)), ((), ())), preferred_element_type=jnp.float32
    )


def tail_product(first, second):
    return lax.dot_general(
        first, second, (((1,), (1,)), ((), ())), preferred_element_type=jnp.float32
    )


def body(
    tile_basis,
    tile_coeffs,
    panel_basis,
    panel_coeffs,
    tile_rank,
    target_rank,
    panel_rank,
    owner_row,
):
    row_basis, row_coeffs = (
        lax.all_gather(panel_basis, "col", axis=1, tiled=True),
        lax.all_gather(panel_coeffs, "col", axis=1, tiled=True),
    )
    source = owner_row[lax.axis_index("col")]
    col_basis, col_coeffs = (spread(row_basis, "row", source), spread(row_coeffs, "row", source))
    here_rank = panel_rank[lax.axis_index("row")]
    there_rank = panel_rank[source]
    left_u = keep_rows(row_basis[0], here_rank)
    left_v = keep_rows(row_coeffs[0], here_rank)
    other_u = keep_rows(col_basis[0], there_rank)
    other_v = keep_rows(col_coeffs[0], there_rank)
    old_rank = tile_rank[0, 0]
    goal_rank = target_rank[0, 0]
    basis = keep_columns(tile_basis[0, 0], old_rank)
    coeffs = keep_columns(tile_coeffs[0, 0], old_rank)
    coupling = tail_product(left_v, other_v).astype(jnp.bfloat16)
    shifted = lead_product(left_u, coupling).astype(jnp.bfloat16)
    sketch = keep_columns(coeffs, goal_rank)
    core_upper = lead_product(coeffs, sketch).astype(jnp.bfloat16)
    core_lower = jnp.dot(other_u, sketch, preferred_element_type=jnp.float32).astype(jnp.bfloat16)
    sampled = jnp.dot(basis, core_upper, preferred_element_type=jnp.float32) - jnp.dot(
        shifted, core_lower, preferred_element_type=jnp.float32
    )
    extra = (jnp.arange(sampled.shape[1]) >= goal_rank).astype(jnp.float32)
    gram_matrix = lax.dot_general(
        sampled,
        sampled,
        (((0,), (0,)), ((), ())),
        precision=lax.Precision.HIGHEST,
        preferred_element_type=jnp.float32,
    )
    gram_matrix = gram_matrix + jnp.diag(extra)
    factor = jnp.linalg.cholesky(gram_matrix)
    orthonormal = jax.scipy.linalg.solve_triangular(factor, sampled.T, lower=True).T
    scaling = math.sqrt(NB)
    fresh_basis = (orthonormal * scaling).astype(jnp.bfloat16)
    reduced_upper = (lead_product(basis, fresh_basis) / scaling).astype(jnp.bfloat16)
    reduced_lower = (-lead_product(shifted, fresh_basis) / scaling).astype(jnp.bfloat16)
    fresh_coeffs = jnp.dot(
        coeffs, reduced_upper, preferred_element_type=jnp.float32
    ) + lead_product(other_u, reduced_lower)
    return (fresh_basis[None, None], fresh_coeffs.astype(jnp.bfloat16)[None, None])


def solution(mesh):
    return jax.shard_map(
        body,
        mesh=mesh,
        in_specs=(
            P("row", "col", None, None),
            P("row", "col", None, None),
            P("row", "col", None),
            P("row", "col", None),
            P("row", "col"),
            P("row", "col"),
            P(),
            P(),
        ),
        out_specs=(P("row", "col", None, None), P("row", "col", None, None)),
        check_vma=False,
    )
```

profile of v0, /device:TPU:0, one launch (start us, length us, event | category | flops | bytes accessed | tf_op | source)
XLA Modules:
  0.0 263.1 jit_solution(7175004458664713414)
XLA Ops:
  7.2 0.7 all-gather.3.cloned.1.call-update
  7.9 0.7 all-gather.5.cloned.1.call-update
  8.7 1.3 dynamic_slice.10
  10.6 19.1 %all-gather.3.cloned.1.call-done = bf16[1,256,2304]{2,1,0:T(8,128)(2,1)} async-done(((bf16[1,64,2304]{2,1,0:T(8,128)(2,1)}), bf16[1,256,2304]{2,1,0:T(8,128)(2,1)}) %all-gather.3.cloned.1.call-update) | async-done | bytes 1179664 | tf_op jit(solution)/shard_map/all_gather | solution.py:48
  29.7 1.1 broadcast_select_fusion
  30.8 18.0 %all-gather.5.cloned.1.call-done = bf16[1,256,2304]{2,1,0:T(8,128)(2,1)} async-done(((bf16[1,64,2304]{2,1,0:T(8,128)(2,1)}), bf16[1,256,2304]{2,1,0:T(8,128)(2,1)}) %all-gather.5.cloned.1.call-update) | async-done | bytes 1179664 | tf_op jit(solution)/shard_map/all_gather | solution.py:49
  48.8 1.1 broadcast_select_fusion.1
  53.3 0.6 fusion.93
  54.5 1.7 compare_convert_fusion.1
  56.2 2.9 %fusion.38 = f32[2304,256]{1,0:T(8,128)} fusion(bf16[1,1,2304,256]{3,2,1,0:T(8,128)(2,1)S(1)} %copy-done.6, bf16[1,1,2304,256]{3,2,1,0:T(8,128)(2,1)S(1)} %copy-done.2, bf16[256]{0:T(256)(128)(2,1)S(1)} %get-tuple-element.32, bf16[256]{0:T(256)(128)(2,1)S(1)} %get-tuple-element.33), kind=kOutput, calls=%fused_computation.39 | convolution fusion | flops 606404608 | bytes 4719616 | tf_op jit(solution)/shard_map/dot_general | solution.py:68
  59.1 102.9 %all-reduce.4.cloned.1.call-done = (bf16[1,256,2304]{2,1,0:T(8,128)(2,1)}, bf16[1,256,2304]{2,1,0:T(8,128)(2,1)}) async-done(((bf16[1,256,2304]{2,1,0:T(8,128)(2,1)}, bf16[1,256,2304]{2,1,0:T(8,128)(2,1)}), (bf16[1,256,2304]{2,1,0:T(8,128)(2,1)}, bf16[1,256,2304]{2,1,0:T(8,128)(2,1)})) %all-reduce.4.cloned.1.call-update) | async-done | bytes 2359312 | tf_op jit(solution)/shard_map/psum | solution.py:12
  162.1 4.3 %convolution_convert_fusion = bf16[2304,256]{1,0:T(8,128)(2,1)} fusion(bf16[1,256,2304]{2,1,0:T(8,128)(2,1)S(1)} %copy-done.5, bf16[1,256,2304]{2,1,0:T(8,128)(2,1)} %get-tuple-element.20, bf16[1,256,2304]{2,1,0:T(8,128)(2,1)} %all-gather.5.cloned.1.call-done, bf16[256]{0:T(256)(128)(2,1)S(1)} %get-tuple-element.34, bf16[256]{0:T(256)(128)(2,1)} %get-tuple-element.35), kind=kOutput, calls=%fused_computation.5 | convolution fusion | flops 606404608 | bytes 4719616 | tf_op jit(solution)/shard_map/dot_general | solution.py:26
  166.4 3.9 %convolution_subtract_fusion = f32[2304,256]{1,0:T(8,128)S(1)} fusion(f32[2304,256]{1,0:T(8,128)} %fusion.38, bf16[2304,256]{1,0:T(8,128)(2,1)} %convolution_convert_fusion, bf16[1,256,2304]{2,1,0:T(8,128)(2,1)S(1)} %copy-done, bf16[1,1,2304,256]{3,2,1,0:T(8,128)(2,1)} %param.9, bf16[256]{0:T(256)(128)(2,1)S(1)} %get-tuple-element.34, ...), kind=kOutput, calls=%fused_computation.3 | convolution fusion | flops 606404608 | bytes 8259072 | tf_op jit(solution)/shard_map/dot_general | solution.py:68
  170.4 3.9 %fusion.94 = f32[256,256]{1,0:T(8,128)S(1)} fusion(f32[2304,256]{1,0:T(8,128)S(1)} %convolution_subtract_fusion), kind=kOutput, calls=%fused_computation.92 | convolution fusion | flops 1811939328 | bytes 2621440 | tf_op jit(solution)/shard_map/dot_general | solution.py:72
  174.5 11.7 %cholesky.49 = f32[128,128]{1,0:T(8,128)S(1)} custom-call(f32[128,128]{1,0:T(8,128)S(1)} %cholesky.115), custom_call_target="Cholesky" | custom-call | tf_op jit(solution)/shard_map/jit(cholesky)/cholesky | solution.py:80
  186.3 9.9 %custom-call.15 = f32[1,128,128]{1,2,0:T(8,128)S(1)} custom-call(f32[1,128,128]{2,1,0:T(8,128)S(1)} %get-tuple-element.27), custom_call_target="InvertDiagBlocksLowerTriangular" | custom-call | tf_op jit(solution)/shard_map/jit(cholesky)/cholesky | solution.py:80
  196.7 11.7 %cholesky.103 = f32[128,128]{1,0:T(8,128)S(1)} custom-call(f32[128,128]{1,0:T(8,128)S(1)} %convolution_subtract_fusion.2), custom_call_target="Cholesky" | custom-call | tf_op jit(solution)/shard_map/jit(cholesky)/cholesky | solution.py:80
  208.4 0.7 compare_reduce_fusion
  209.1 0.6 compare_reduce_fusion.1
  211.1 5.2 %while.1 = (s32[]{:T(128)}, f32[256,256]{1,0:T(8,128)S(1)}, s32[2,2]{1,0:T(2,128)S(1)}, f32[2,128,128]{2,1,0:T(8,128)}, s32[]{:T(128)}) while((s32[]{:T(128)}, f32[256,256]{1,0:T(8,128)S(1)}, s32[2,2]{1,0:T(2,128)S(1)}, f32[2,128,128]{2,1,0:T(8,128)}, s32[]{:T(128)}) %tuple.30), condition=%wide.while_cond, body=%wide.while_body.sunk | while | flops 2 | bytes 132705 | solution.py:81
  211.1 0.6 fusion.104
  211.7 2.0 bitcast_dynamic-update-slice_fusion.2
  213.7 0.6 fusion.104
  214.3 2.0 bitcast_dynamic-update-slice_fusion.2
  216.3 21.2 %custom-call.16 = f32[2,128,128]{1,2,0:T(8,128)} custom-call(f32[2,128,128]{2,1,0:T(8,128)} %get-tuple-element.9), custom_call_target="InvertDiagBlocksLowerTriangular" | custom-call | tf_op jit(solution)/shard_map/jit(_solve_triangular)/triangular_solve | solution.py:81
  237.5 2.0 fusion.3
  239.5 2.9 %convolution_subtract_fusion.1 = f32[128,2304]{0,1:T(8,128)S(1)} fusion(f32[128,2304]{1,0:T(8,128)S(1)} %fusion.3, f32[256,2304]{0,1:T(8,128)S(1)} %bitcast.108, f32[256,256]{1,0:T(8,128)} %copy-done.4), kind=kOutput, calls=%fused_computation.6 | convolution fusion | flops 453279744 | bytes 3604480 | tf_op jit(solution)/shard_map/jit(_solve_triangular)/triangular_solve | solution.py:81
  242.4 1.2 fusion.81
  243.7 4.2 %fusion.5 = f32[2304,256]{1,0:T(8,128)} fusion(bf16[1,1,2304,256]{3,2,1,0:T(8,128)(2,1)S(1)} %copy-done.3, bf16[1,1,2304,256]{3,2,1,0:T(8,128)(2,1)} %param.8, bf16[256]{0:T(256)(128)(2,1)S(1)} %get-tuple-element.33, f32[128,2304]{1,0:T(8,128)S(1)} %fusion.81, f32[128,2304]{1,0:T(8,128)S(1)} %fusion.3), kind=kOutput, calls=%fused_computation.14 | convolution fusion | flops 607059968 | bytes 7078400 | tf_op jit(solution)/shard_map/dot_general | solution.py:86
  247.9 1.2 fusion.91
  249.6 4.6 %fusion.1 = bf16[1,1,2304,256]{3,2,1,0:T(8,128)(2,1)} fusion(f32[2304,256]{1,0:T(8,128)} %fusion.5, bf16[1,256,2304]{2,1,0:T(8,128)(2,1)S(1)} %copy-done.1, bf16[2304,256]{1,0:T(8,128)(2,1)} %convolution_convert_fusion, bf16[256]{0:T(256)(128)(2,1)S(1)} %get-tuple-element.34, f32[128,2304]{1,0:T(8,128)S(1)} %fusion.81, f32[128,2304]{1,0:T(8,128)S(1)} %fusion.3), kind=kOutput, calls=%fused_computation.7 | convolution fusion | flops 607715328 | bytes 8258048 | tf_op jit(solution)/shard_map/dot_general | solution.py:26
  254.2 2.4 copy.11
  (40 shorter events, 2.3 us)
Async XLA Ops:
  7.2 22.6 %all-gather.3.cloned.1.call-start = ((), (), s32[]{:S(2)}) async-start(), calls=%async_computation | async-start | bytes 1474560 | tf_op jit(solution)/shard_map/all_gather | solution.py:48
  7.9 40.9 %all-gather.5.cloned.1.call-start = ((), (), s32[]{:S(2)}) async-start(), calls=%async_computation.1 | async-start | bytes 1474560 | tf_op jit(solution)/shard_map/all_gather | solution.py:49
  8.6 153.4 %all-reduce.4.cloned.1.call-start = ((), (), s32[]{:S(2)}) async-start(), calls=%async_computation.2 | async-start | bytes 4718592 | tf_op jit(solution)/shard_map/psum | solution.py:12
  49.9 3.4 %copy-start.8 = (s32[8]{0:T(128)S(1)}, s32[8]{0:T(128)}, u32[]{:S(2)}) copy-start(s32[8]{0:T(128)} %param.14) | copy-start | bytes 100
  49.9 6.3 %copy-start.2 = (bf16[1,1,2304,256]{3,2,1,0:T(8,128)(2,1)S(1)}, bf16[1,1,2304,256]{3,2,1,0:T(8,128)(2,1)}, u32[]{:S(2)}) copy-start(bf16[1,1,2304,256]{3,2,1,0:T(8,128)(2,1)} %param.9) | copy-start | bytes 3538948
  49.9 6.3 %copy-start.6 = (bf16[1,1,2304,256]{3,2,1,0:T(8,128)(2,1)S(1)}, bf16[1,1,2304,256]{3,2,1,0:T(8,128)(2,1)}, u32[]{:S(2)}) copy-start(bf16[1,1,2304,256]{3,2,1,0:T(8,128)(2,1)} %param.8) | copy-start | bytes 3538948
  56.2 105.9 %copy-start.5 = (bf16[1,256,2304]{2,1,0:T(8,128)(2,1)S(1)}, bf16[1,256,2304]{2,1,0:T(8,128)(2,1)}, u32[]{:S(2)}) copy-start(bf16[1,256,2304]{2,1,0:T(8,128)(2,1)} %all-gather.3.cloned.1.call-done) | copy-start | bytes 3538948
  162.1 4.3 %copy-start = (bf16[1,256,2304]{2,1,0:T(8,128)(2,1)S(1)}, bf16[1,256,2304]{2,1,0:T(8,128)(2,1)}, u32[]{:S(2)}) copy-start(bf16[1,256,2304]{2,1,0:T(8,128)(2,1)} %get-tuple-element.21) | copy-start | bytes 3538948
  174.4 36.7 %copy-start.9 = (s32[2]{0:T(128)S(1)}, s32[2]{0:T(128)}, u32[]{:S(2)}) copy-start(s32[2]{0:T(128)} %iota_multiply_fusion) | copy-start | bytes 28
  216.3 21.2 %copy-start.4 = (f32[256,256]{1,0:T(8,128)}, f32[256,256]{1,0:T(8,128)S(1)}, u32[]{:S(2)}) copy-start(f32[256,256]{1,0:T(8,128)S(1)} %get-tuple-element.91) | copy-start | bytes 786436
  239.5 2.9 %copy-start.7 = (f32[2,128,128]{1,2,0:T(8,128)S(1)}, f32[2,128,128]{1,2,0:T(8,128)}, u32[]{:S(2)}) copy-start(f32[2,128,128]{1,2,0:T(8,128)} %custom-call.16) | copy-start | bytes 393220
  242.4 1.3 copy-start.3
  247.9 1.7 copy-start.1
Sparse Core Ops, SparseCore 0:
  9.6 20.1 all-gather.2
  31.3 17.4 all-gather.4
  53.0 109.0 all-reduce.3
where the time goes:
time: 264 us; the launch traced here: 263 us
  waiting for transfers between devices  141 us (53%)
  other arithmetic  61.6 us (23%)
  matrix products  30.4 us (12%)
  between operations  19.2 us (7%)
  local copies, waits for them, and re-layouts  10.3 us (4%)
    psum x1, waiting for transfers between devices, spread(): return lax.psum(kept, axis)  103 us
    another operation x7, other arithmetic, body(): factor = jnp.linalg.cholesky(gram_matrix)  34.7 us
    another operation x3, other arithmetic, body(): jax.scipy.linalg.solve_triangular(factor, sampled.T, lower=True)  21.8 us
    all_gather x1, waiting for transfers between devices, body(): lax.all_gather(panel_basis, 'col', axis=1, tiled=True)  19.1 us
    all_gather x1, waiting for transfers between devices, body(): lax.all_gather(panel_coeffs, 'col', axis=1, tiled=True)  18 us
    dot_general x2, matrix products, lead_product(): lax.dot_general(first, second, (((0,), (0,)), ((), ())), preferred_elemen...  8.91 us
    another operation x3, matrix products, body(): jax.scipy.linalg.solve_triangular(factor, sampled.T, lower=True)  6.08 us
  transfers between devices with their start and end apart: 3, of which 3 were waited for; matrix products, arithmetic and copies ran while one was open for 3% of the time, Pallas kernels for 0%

commit v1 on v0

--- a/solution.py
+++ b/solution.py
@@ -5,6 +5,19 @@
 from jax.sharding import PartitionSpec as P
 
 NB = 2304
+
+
+def gather_around(value, axis, dim):
+    ways = lax.axis_size(axis)
+    up = [(d, (d + 1) % ways) for d in range(ways)]
+    down = [(d, (d - 1) % ways) for d in range(ways)]
+    earlier, later = ([value], [value])
+    for _ in range(ways // 2):
+        earlier.append(lax.ppermute(earlier[-1], axis, up))
+    for _ in range((ways - 1) // 2):
+        later.append(lax.ppermute(later[-1], axis, down))
+    line = jnp.concatenate([*earlier[::-1], *later[1:]], axis=dim)
+    return jnp.roll(line, (lax.axis_index(axis) - ways // 2) * value.shape[dim], axis=dim)
 
 
 def spread(value, axis, source):
@@ -46,7 +59,7 @@
 ):
     row_basis, row_coeffs = (
         lax.all_gather(panel_basis, "col", axis=1, tiled=True),
-        lax.all_gather(panel_coeffs, "col", axis=1, tiled=True),
+        gather_around(panel_coeffs, "col", 1),
     )
     source = owner_row[lax.axis_index("col")]
     col_basis, col_coeffs = (spread(row_basis, "row", source), spread(row_coeffs, "row", source))

time: 264 us -> 251 us (0.951)
  waiting for transfers between devices: 141 us -> 124 us
    all_gather x1 -> x0, waiting for transfers between devices: 18 us -> none  [body(): lax.all_gather(panel_coeffs, 'col', axis=1, tiled=True)]
    ppermute x0 -> x3, waiting for transfers between devices: none -> 11.9 us  [the longest x2 9.15 us: gather_around(): earlier.append(lax.ppermute(earlier[-1], axis, up))]
    all_gather x1, waiting for transfers between devices: 19.1 us -> 9.42 us  [body(): lax.all_gather(panel_basis, 'col', axis=1, tiled=True)]
  transfers between devices with their start and end apart: 3 -> 5, of which waited for: 3 -> 5; matrix products, arithmetic and copies ran while one was open for 3% -> 3% of each run, Pallas kernels for 0% -> 0%
where the time goes in v1:
time: 251 us; the launch traced here: 250 us
  waiting for transfers between devices  124 us (49%)
  other arithmetic  61.8 us (25%)
  matrix products  30.4 us (12%)
  between operations  19.7 us (8%)
  local copies, waits for them, and re-layouts  12 us (5%)
    psum x1, waiting for transfers between devices, spread(): return lax.psum(kept, axis)  103 us
    another operation x7, other arithmetic, body(): factor = jnp.linalg.cholesky(gram_matrix)  34.7 us
    another operation x3, other arithmetic, body(): jax.scipy.linalg.solve_triangular(factor, sampled.T, lower=True)  21.7 us
    all_gather x1, waiting for transfers between devices, body(): lax.all_gather(panel_basis, 'col', axis=1, tiled=True)  9.42 us
    ppermute x2, waiting for transfers between devices, gather_around(): earlier.append(lax.ppermute(earlier[-1], axis, up))  9.15 us
    dot_general x2, matrix products, lead_product(): lax.dot_general(first, second, (((0,), (0,)), ((), ())), preferred_elemen...  8.91 us
    another operation x3, matrix products, body(): jax.scipy.linalg.solve_triangular(factor, sampled.T, lower=True)  6.08 us
    another operation x6, local copies, waits for them, and re-layouts  5.17 us
  transfers between devices with their start and end apart: 5, of which 5 were waited for; matrix products, arithmetic and copies ran while one was open for 3% of the time, Pallas kernels for 0%

profile of v1, /device:TPU:0, one launch (start us, length us, event | category | flops | bytes accessed | tf_op | source)
XLA Modules:
  0.0 250.5 jit_solution(17720448582142560657)
XLA Ops:
  7.7 6.5 %collective-permute-done = bf16[1,64,2304]{2,1,0:T(8,128)(2,1)S(1)} collective-permute-done((bf16[1,64,2304]{2,1,0:T(8,128)(2,1)}, bf16[1,64,2304]{2,1,0:T(8,128)(2,1)S(1)}, u32[]{:S(2)}, u32[]{:S(2)}) %collective-permute-start) | collective-permute-done | bytes 294944 | tf_op jit(solution)/shard_map/ppermute | solution.py:16
  14.3 1.7 collective-permute-start.2
  16.1 1.3 dynamic_slice.15
  18.1 2.6 %collective-permute-done.1 = bf16[1,64,2304]{2,1,0:T(8,128)(2,1)S(1)} collective-permute-done((bf16[1,64,2304]{2,1,0:T(8,128)(2,1)S(1)}, bf16[1,64,2304]{2,1,0:T(8,128)(2,1)S(1)}, u32[]{:S(2)}, u32[]{:S(2)}) %collective-permute-start.1) | collective-permute-done | bytes 294944 | tf_op jit(solution)/shard_map/ppermute | solution.py:16
  20.8 2.7 %collective-permute-done.2 = bf16[1,64,2304]{2,1,0:T(8,128)(2,1)S(1)} collective-permute-done((bf16[1,64,2304]{2,1,0:T(8,128)(2,1)}, bf16[1,64,2304]{2,1,0:T(8,128)(2,1)S(1)}, u32[]{:S(2)}, u32[]{:S(2)}) %collective-permute-start.2) | collective-permute-done | bytes 294944 | tf_op jit(solution)/shard_map/ppermute | solution.py:18
  23.7 1.4 copy-done.8
  25.1 1.2 broadcast_select_fusion.1
  26.3 9.4 %all-gather.2.cloned.1.call-done = bf16[1,256,2304]{2,1,0:T(8,128)(2,1)} async-done(((bf16[1,64,2304]{2,1,0:T(8,128)(2,1)}), bf16[1,256,2304]{2,1,0:T(8,128)(2,1)}) %all-gather.2.cloned.1.call-update) | async-done | bytes 1179664 | tf_op jit(solution)/shard_map/all_gather | solution.py:61
  35.7 1.1 broadcast_select_fusion
  40.3 0.7 fusion.96
  41.5 1.8 compare_convert_fusion.1
  43.4 2.9 %fusion.38 = f32[2304,256]{1,0:T(8,128)} fusion(bf16[1,1,2304,256]{3,2,1,0:T(8,128)(2,1)S(1)} %copy-done.7, bf16[1,1,2304,256]{3,2,1,0:T(8,128)(2,1)S(1)} %copy-done.2, bf16[256]{0:T(256)(128)(2,1)S(1)} %get-tuple-element.32, bf16[256]{0:T(256)(128)(2,1)S(1)} %get-tuple-element.33), kind=kOutput, calls=%fused_computation.39 | convolution fusion | flops 606404608 | bytes 4719616 | tf_op jit(solution)/shard_map/dot_general | solution.py:81
  46.3 102.7 %all-reduce.4.cloned.1.call-done = (bf16[1,256,2304]{2,1,0:T(8,128)(2,1)}, bf16[1,256,2304]{2,1,0:T(8,128)(2,1)}) async-done(((bf16[1,256,2304]{2,1,0:T(8,128)(2,1)}, bf16[1,256,2304]{2,1,0:T(8,128)(2,1)}), (bf16[1,256,2304]{2,1,0:T(8,128)(2,1)}, bf16[1,256,2304]{2,1,0:T(8,128)(2,1)})) %all-reduce.4.cloned.1.call-update) | async-done | bytes 2359312 | tf_op jit(solution)/shard_map/psum | solution.py:25
  149.0 4.3 %convolution_convert_fusion = bf16[2304,256]{1,0:T(8,128)(2,1)} fusion(bf16[1,256,2304]{2,1,0:T(8,128)(2,1)S(1)} %copy-done.5, bf16[1,256,2304]{2,1,0:T(8,128)(2,1)} %get-tuple-element.20, bf16[1,512,2304]{2,1,0:T(8,128)(2,1)} %copy-done.8, s32[]{:T(128)S(6)} %select_n.48, bf16[256]{0:T(256)(128)(2,1)S(1)} %get-tuple-element.34, ...), kind=kOutput, calls=%fused_computation.5 | convolution fusion | flops 608174080 | bytes 4720132 | tf_op jit(solution)/shard_map/dot_general | solution.py:39
  153.3 3.9 %convolution_subtract_fusion = f32[2304,256]{1,0:T(8,128)S(1)} fusion(f32[2304,256]{1,0:T(8,128)} %fusion.38, bf16[2304,256]{1,0:T(8,128)(2,1)} %convolution_convert_fusion, bf16[1,256,2304]{2,1,0:T(8,128)(2,1)S(1)} %copy-done, bf16[1,1,2304,256]{3,2,1,0:T(8,128)(2,1)} %param.9, bf16[256]{0:T(256)(128)(2,1)S(1)} %get-tuple-element.34, ...), kind=kOutput, calls=%fused_computation.3 | convolution fusion | flops 606404608 | bytes 8259072 | tf_op jit(solution)/shard_map/dot_general | solution.py:81
  157.3 3.9 %fusion.97 = f32[256,256]{1,0:T(8,128)S(1)} fusion(f32[2304,256]{1,0:T(8,128)S(1)} %convolution_subtract_fusion), kind=kOutput, calls=%fused_computation.102 | convolution fusion | flops 1811939328 | bytes 2621440 | tf_op jit(solution)/shard_map/dot_general | solution.py:85
  161.4 11.8 %cholesky.49 = f32[128,128]{1,0:T(8,128)S(1)} custom-call(f32[128,128]{1,0:T(8,128)S(1)} %cholesky.115), custom_call_target="Cholesky" | custom-call | tf_op jit(solution)/shard_map/jit(cholesky)/cholesky | solution.py:93
  173.3 9.8 %custom-call.15 = f32[1,128,128]{1,2,0:T(8,128)S(1)} custom-call(f32[1,128,128]{2,1,0:T(8,128)S(1)} %get-tuple-element.27), custom_call_target="InvertDiagBlocksLowerTriangular" | custom-call | tf_op jit(solution)/shard_map/jit(cholesky)/cholesky | solution.py:93
  183.6 11.7 %cholesky.103 = f32[128,128]{1,0:T(8,128)S(1)} custom-call(f32[128,128]{1,0:T(8,128)S(1)} %convolution_subtract_fusion.2), custom_call_target="Cholesky" | custom-call | tf_op jit(solution)/shard_map/jit(cholesky)/cholesky | solution.py:93
  195.3 0.7 compare_reduce_fusion
  196.0 0.6 compare_reduce_fusion.1
  198.0 5.4 %while.1 = (s32[]{:T(128)}, f32[256,256]{1,0:T(8,128)S(1)}, s32[2,2]{1,0:T(2,128)S(1)}, f32[2,128,128]{2,1,0:T(8,128)}, s32[]{:T(128)}) while((s32[]{:T(128)}, f32[256,256]{1,0:T(8,128)S(1)}, s32[2,2]{1,0:T(2,128)S(1)}, f32[2,128,128]{2,1,0:T(8,128)}, s32[]{:T(128)}) %tuple.30), condition=%wide.while_cond, body=%wide.while_body.sunk | while | flops 2 | bytes 132705 | solution.py:94
  198.8 2.0 bitcast_dynamic-update-slice_fusion.2
  201.4 2.0 bitcast_dynamic-update-slice_fusion.2
  203.4 21.2 %custom-call.16 = f32[2,128,128]{1,2,0:T(8,128)} custom-call(f32[2,128,128]{2,1,0:T(8,128)} %get-tuple-element.9), custom_call_target="InvertDiagBlocksLowerTriangular" | custom-call | tf_op jit(solution)/shard_map/jit(_solve_triangular)/triangular_solve | solution.py:94
  224.6 2.0 fusion.3
  226.6 2.9 %convolution_subtract_fusion.1 = f32[128,2304]{0,1:T(8,128)S(1)} fusion(f32[128,2304]{1,0:T(8,128)S(1)} %fusion.3, f32[256,2304]{0,1:T(8,128)S(1)} %bitcast.108, f32[256,256]{1,0:T(8,128)} %copy-done.4), kind=kOutput, calls=%fused_computation.6 | convolution fusion | flops 453279744 | bytes 3604480 | tf_op jit(solution)/shard_map/jit(_solve_triangular)/triangular_solve | solution.py:94
  229.5 1.2 fusion.82
  230.8 4.2 %fusion.5 = f32[2304,256]{1,0:T(8,128)} fusion(bf16[1,1,2304,256]{3,2,1,0:T(8,128)(2,1)S(1)} %copy-done.3, bf16[1,1,2304,256]{3,2,1,0:T(8,128)(2,1)} %param.8, bf16[256]{0:T(256)(128)(2,1)S(1)} %get-tuple-element.33, f32[128,2304]{1,0:T(8,128)S(1)} %fusion.82, f32[128,2304]{1,0:T(8,128)S(1)} %fusion.3), kind=kOutput, calls=%fused_computation.14 | convolution fusion | flops 607059968 | bytes 7078400 | tf_op jit(solution)/shard_map/dot_general | solution.py:99
  235.0 1.2 fusion.94
  236.7 4.6 %fusion.1 = bf16[1,1,2304,256]{3,2,1,0:T(8,128)(2,1)} fusion(f32[2304,256]{1,0:T(8,128)} %fusion.5, bf16[1,256,2304]{2,1,0:T(8,128)(2,1)S(1)} %copy-done.1, bf16[2304,256]{1,0:T(8,128)(2,1)} %convolution_convert_fusion, bf16[256]{0:T(256)(128)(2,1)S(1)} %get-tuple-element.34, f32[128,2304]{1,0:T(8,128)S(1)} %fusion.82, f32[128,2304]{1,0:T(8,128)S(1)} %fusion.3), kind=kOutput, calls=%fused_computation.7 | convolution fusion | flops 607715328 | bytes 8258048 | tf_op jit(solution)/shard_map/dot_general | solution.py:39
  241.3 2.4 copy.11
  (55 shorter events, 4.1 us)
Async XLA Ops:
  7.2 13.6 %copy-start.6 = (bf16[1,64,2304]{2,1,0:T(8,128)(2,1)S(1)}, bf16[1,64,2304]{2,1,0:T(8,128)(2,1)}, u32[]{:S(2)}) copy-start(bf16[1,64,2304]{2,1,0:T(8,128)(2,1)} %param.11) | copy-start | bytes 884740
  7.2 28.5 %all-gather.2.cloned.1.call-start = ((), (), s32[]{:S(2)}) async-start(), calls=%async_computation | async-start | bytes 1474560 | tf_op jit(solution)/shard_map/all_gather | solution.py:61
  7.2 7.0 %collective-permute-start = (bf16[1,64,2304]{2,1,0:T(8,128)(2,1)}, bf16[1,64,2304]{2,1,0:T(8,128)(2,1)S(1)}, u32[]{:S(2)}, u32[]{:S(2)}) collective-permute-start(bf16[1,64,2304]{2,1,0:T(8,128)(2,1)} %param.11), channel_id=1, source_target_pairs={{0,1},{1,2},{2,3},{3,0},{4,5},{5,6},{6,7},{7,4},{8,9},{9,10},{10,1... | collective-permute-start | bytes 884744 | tf_op jit(solution)/shard_map/ppermute | solution.py:16
  14.3 6.4 %collective-permute-start.1 = (bf16[1,64,2304]{2,1,0:T(8,128)(2,1)S(1)}, bf16[1,64,2304]{2,1,0:T(8,128)(2,1)S(1)}, u32[]{:S(2)}, u32[]{:S(2)}) collective-permute-start(bf16[1,64,2304]{2,1,0:T(8,128)(2,1)S(1)} %collective-permute-done), channel_id=1, source_target_pairs={{0,1},{1,2},{2,3},{3,0},{4,5},{5,6},{6,7},{7,4},{8,9},{9,10},{10,1... | collective-permute-start | bytes 884744 | tf_op jit(solution)/shard_map/ppermute | solution.py:16
  14.3 9.2 %collective-permute-start.2 = (bf16[1,64,2304]{2,1,0:T(8,128)(2,1)}, bf16[1,64,2304]{2,1,0:T(8,128)(2,1)S(1)}, u32[]{:S(2)}, u32[]{:S(2)}) collective-permute-start(bf16[1,64,2304]{2,1,0:T(8,128)(2,1)} %param.11), channel_id=1, source_target_pairs={{0,3},{1,0},{2,1},{3,2},{4,7},{5,4},{6,5},{7,6},{8,11},{9,8},{10,9... | collective-permute-start | bytes 884744 | tf_op jit(solution)/shard_map/ppermute | solution.py:18
  16.0 133.0 %all-reduce.4.cloned.1.call-start = ((), (), s32[]{:S(2)}) async-start(), calls=%async_computation.1 | async-start | bytes 4718592 | tf_op jit(solution)/shard_map/psum | solution.py:25
  23.6 1.4 copy-start.8
  36.8 3.5 %copy-start.10 = (s32[8]{0:T(128)S(1)}, s32[8]{0:T(128)}, u32[]{:S(2)}) copy-start(s32[8]{0:T(128)} %param.14) | copy-start | bytes 100
  36.8 6.6 %copy-start.2 = (bf16[1,1,2304,256]{3,2,1,0:T(8,128)(2,1)S(1)}, bf16[1,1,2304,256]{3,2,1,0:T(8,128)(2,1)}, u32[]{:S(2)}) copy-start(bf16[1,1,2304,256]{3,2,1,0:T(8,128)(2,1)} %param.9) | copy-start | bytes 3538948
  36.8 6.6 %copy-start.7 = (bf16[1,1,2304,256]{3,2,1,0:T(8,128)(2,1)S(1)}, bf16[1,1,2304,256]{3,2,1,0:T(8,128)(2,1)}, u32[]{:S(2)}) copy-start(bf16[1,1,2304,256]{3,2,1,0:T(8,128)(2,1)} %param.8) | copy-start | bytes 3538948
  43.4 105.6 %copy-start.5 = (bf16[1,256,2304]{2,1,0:T(8,128)(2,1)S(1)}, bf16[1,256,2304]{2,1,0:T(8,128)(2,1)}, u32[]{:S(2)}) copy-start(bf16[1,256,2304]{2,1,0:T(8,128)(2,1)} %all-gather.2.cloned.1.call-done) | copy-start | bytes 3538948
  149.0 4.3 %copy-start = (bf16[1,256,2304]{2,1,0:T(8,128)(2,1)S(1)}, bf16[1,256,2304]{2,1,0:T(8,128)(2,1)}, u32[]{:S(2)}) copy-start(bf16[1,256,2304]{2,1,0:T(8,128)(2,1)} %get-tuple-element.21) | copy-start | bytes 3538948
  161.3 36.7 %copy-start.11 = (s32[2]{0:T(128)S(1)}, s32[2]{0:T(128)}, u32[]{:S(2)}) copy-start(s32[2]{0:T(128)} %iota_multiply_fusion) | copy-start | bytes 28
  203.4 21.2 %copy-start.4 = (f32[256,256]{1,0:T(8,128)}, f32[256,256]{1,0:T(8,128)S(1)}, u32[]{:S(2)}) copy-start(f32[256,256]{1,0:T(8,128)S(1)} %get-tuple-element.90) | copy-start | bytes 786436
  226.6 2.9 %copy-start.9 = (f32[2,128,128]{1,2,0:T(8,128)S(1)}, f32[2,128,128]{1,2,0:T(8,128)}, u32[]{:S(2)}) copy-start(f32[2,128,128]{1,2,0:T(8,128)} %custom-call.16) | copy-start | bytes 393220
  229.5 1.3 copy-start.3
  235.0 1.7 copy-start.1
Sparse Core Ops, SparseCore 0:
  16.2 19.5 all-gather.1
  39.9 109.0 all-reduce.3
